TPU v7x, 128 devices: a whole 4x4x4 slice. The times are simulated.
128 devices in a mesh: visit: 4 (over x), patch: 32 (over z, y, core).
Axes of the slice: x: 4, y: 4, z: 4, core: 2. Of those that a mesh axis runs over, the one named last changes fastest.
Arguments:
- image: float32 [4096, 128, 128], P(('visit', 'patch')), may hold values from -6 to 6
- variance: float32 [4096, 128, 128], P(('visit', 'patch')), may hold values from 0.25 to 4
- intersections: int32 [4096, 2], P(('visit', 'patch')), may hold values from 0 to 31, all different within a row; in each aligned block of 32 rows (0 to 31, 32 to 63, ...) at most 3 rows name the same one
- boxes: int32 [4096, 2, 2], P(('visit', 'patch')), may hold values from -64 to 191
- shifts: float32 [4096, 2, 2], P(('visit', 'patch')), may hold values from 0 to 1
- basis_ids: int32 [4096, 3], P(('visit', 'patch')), may hold values from 0 to 7
- coefs: float32 [4096, 3], P(('visit', 'patch')), may hold values from 0.3 to 1.5
- taps: float32 [8, 2, 41], replicated, may hold values from -1 to 1
Outputs:
- coadd: float32 [8192, 256], P('patch')
- coadd_var: float32 [8192, 256], P('patch')
Inputs may be any that keep to these rules, and one draw needn't show every extreme that they name: `intersections`: the rows of one device name every patch at most 3 times; each tile names two different patches.
All inputs are finite; a program needn't handle non-finite values.
Results may differ from a plain program's by a relative error of at most 0.0003.
Values sent between devices are 32-bit elements; how exact they have to be, the bound alone decides.
No kernel may reach another device: no remote copies, remote signals or barrier semaphores. Data moves between devices by JAX's collectives and lax.ppermute only.
A program may use at most 128 MiB of HBM per device.

v0:
```python
import jax
import jax.numpy as jnp
from jax import lax
from jax.sharding import PartitionSpec as P

PATCH = 256
HI = lax.Precision.HIGHEST
group_width = 8


def band_table(side, ntaps):
    offs = jnp.arange(side)[:, None] - jnp.arange(side)[None, :] + (ntaps - 1) // 2
    return (offs[:, :, None] == jnp.arange(ntaps)[None, None, :]).astype(jnp.float32)


def convolve(images, row_taps, col_taps, weights_b):
    band = band_table(images.shape[-1], row_taps.shape[-1])
    row_mats = jnp.einsum("ikt,gbt->gbik", band, row_taps, precision=HI)
    col_mats = jnp.einsum("jlt,gbt->gbjl", band, col_taps, precision=HI)
    partial_rows = jnp.einsum("gbik,gkl->gbil", row_mats, images, precision=HI)
    scaled = partial_rows * weights_b[:, :, None, None]
    return jnp.einsum("gbil,gbjl->gij", scaled, col_mats, precision=HI)


def interpolation(offset, shift, count, side):
    place = (
        jnp.arange(count).astype(jnp.float32)[None, :, None]
        - offset[:, None, None]
        - shift[:, None, None]
        - jnp.arange(side).astype(jnp.float32)[None, None, :]
    )
    return jnp.maximum(0.0, 1.0 - jnp.abs(place))


def warp_group(planes, meta, patch_side):
    side = planes.shape[-1]
    rows_w = interpolation(meta[:, 1], meta[:, 3], patch_side, side)
    cols_w = interpolation(meta[:, 2], meta[:, 4], patch_side, side)
    left = jnp.einsum("gpi,gcij->gcpj", rows_w, planes, precision=HI)
    both = jnp.einsum("gcpj,gqj->gcpq", left, cols_w, precision=HI)
    weight = meta[:, 0]
    num = jnp.sum(weight[:, None, None] * both[:, 0], 0)
    vsum = jnp.sum((weight * weight)[:, None, None] * both[:, 1], 0)
    cover = jnp.sum(rows_w, 2)[:, :, None] * jnp.sum(cols_w, 2)[:, None, :]
    den = jnp.sum(weight[:, None, None] * cover, 0)
    return jnp.stack([num, den, vsum], 0)


def finish(num, den, vsum):
    safe = jnp.maximum(den, 1.0)
    return (num / safe, vsum / (safe * safe))


def basis_taps(ids, taps):
    select = (ids[..., None] == jnp.arange(taps.shape[0])[None, None, :]).astype(jnp.float32)
    row_t = jnp.einsum("gbn,nk->gbk", select, taps[:, 0], precision=HI)
    col_t = jnp.einsum("gbn,nk->gbk", select, taps[:, 1], precision=HI)
    return (row_t, col_t)


def shards(image, variance, intersections, boxes, shifts, basis_ids, coefs, taps):
    tiles = image.shape[0]
    side = image.shape[1]
    nterms = coefs.shape[1]
    peers = lax.axis_size("patch")
    capacity = max(2, 3 * tiles // peers)
    slots = peers * capacity
    dest = intersections.reshape(-1)
    count = dest.shape[0]
    order = jnp.arange(count)
    earlier = (dest[:, None] == dest[None, :]) & (order[None, :] < order[:, None])
    rank = jnp.sum(earlier.astype(jnp.int32), 1)
    slot_of = dest * capacity + rank
    match = slot_of[None, :] == jnp.arange(slots)[:, None]
    live = jnp.any(match, 1)
    item = jnp.sum(jnp.where(match, order[None, :], 0), 1)
    tile_of = item // 2
    livef = live.astype(jnp.float32)
    inverse_var = 1.0 / jnp.mean(variance, axis=(1, 2))
    box_flat = boxes.reshape(count, 2).astype(jnp.float32)[item]
    shift_flat = shifts.reshape(count, 2)[item]
    geometry = jnp.concatenate([(inverse_var[tile_of] * livef)[:, None], box_flat, shift_flat], 1)
    planes = jnp.stack([image, variance], 1)[tile_of] * livef[:, None, None, None]
    meta = jnp.concatenate([geometry, coefs[tile_of], basis_ids[tile_of].astype(jnp.float32)], 1)
    width = meta.shape[1]
    sent = planes.reshape(peers, capacity, 2, side, side)
    sent_meta = meta.reshape(peers, capacity, width)
    arrived, arrived_meta = (
        lax.all_to_all(sent, "patch", split_axis=0, concat_axis=0, tiled=True),
        lax.all_to_all(sent_meta, "patch", split_axis=0, concat_axis=0, tiled=True),
    )
    groups = slots // group_width
    arrived = arrived.reshape(groups, group_width, 2, side, side)
    arrived_meta = arrived_meta.reshape(groups, group_width, width)

    def accumulate(total, parts):
        block, block_meta = parts
        ids = block_meta[:, 5 + nterms : 5 + 2 * nterms].astype(jnp.int32)
        row_t, col_t = basis_taps(ids, taps)
        matched = convolve(block[:, 0], row_t, col_t, block_meta[:, 5 : 5 + nterms])
        block = jnp.stack([matched, block[:, 1]], 1)
        return (total + warp_group(block, block_meta, PATCH), None)

    start = jnp.zeros((3, PATCH, PATCH), jnp.float32)
    partial_value = lax.scan(accumulate, start, (arrived, arrived_meta))[0]
    total = lax.psum(partial_value, "visit")
    coadd, coadd_var = finish(total[0], total[1], total[2])
    return (coadd, coadd_var)


def solution(mesh):
    in_specs = (
        P(("visit", "patch"), None, None),
        P(("visit", "patch"), None, None),
        P(("visit", "patch"), None),
        P(("visit", "patch"), None, None),
        P(("visit", "patch"), None, None),
        P(("visit", "patch"), None),
        P(("visit", "patch"), None),
        P(),
    )
    out_specs = (P("patch", None), P("patch", None))
    return jax.shard_map(shards, mesh=mesh, in_specs=in_specs, out_specs=out_specs, check_vma=False)
```

profile of v0, /device:TPU:0, one launch (start us, length us, event | category | flops | bytes accessed | tf_op | source)
XLA Modules:
  0.0 473.0 jit_solution(7930241180158183529)
XLA Ops:
  8.5 1.9 reduce_sum.75
  16.5 8.4 %all-to-all-start = ((f32[32,3,11]{2,1,0:T(4,128)}), f32[32,3,11]{2,1,0:T(4,128)S(1)}, u32[]{:S(2)}, u32[]{:S(2)}) async-start(f32[32,3,11]{2,1,0:T(4,128)} %copy.90), calls=%async_computation | async-start | bytes 131072 | tf_op jit(solution)/shard_map/all_to_all | solution.py:90
  24.9 3.9 pad_maximum_fusion.1
  28.9 10.9 %gather_fusion.5 = f32[96,2,128,128]{3,2,1,0:T(8,128)} fusion(f32[32,2,128,128]{3,2,0,1:T(8,128)} %pad_maximum_fusion.1, s32[1024]{0:T(1024)S(1)} %get-tuple-element.97), kind=kCustom, calls=%fused_computation.5 | custom fusion | bytes 25166208 | tf_op jit(solution)/shard_map/gather | solution.py:83
  39.9 11.8 %broadcast_multiply_fusion = f32[32,3,2,128,128]{4,3,2,1,0:T(8,128)} fusion(f32[32,3,2,128,128]{4,3,2,1,0:T(8,128)} %bitcast.135, f32[32,3]{1,0:T(8,128)S(1)} %reshape.285), kind=kLoop, calls=%fused_computation.74 | loop fusion | flops 3145728 | bytes 25166208 | tf_op jit(solution)/shard_map/mul | solution.py:83
  51.6 7.6 %all-to-all-start.1 = ((f32[32,3,2,128,128]{4,3,2,1,0:T(8,128)}), f32[32,3,2,128,128]{4,3,2,1,0:T(8,128)}, u32[]{:S(2)}, u32[]{:S(2)}) async-start(f32[32,3,2,128,128]{4,3,2,1,0:T(8,128)} %broadcast_multiply_fusion), calls=%async_computation.1 | async-start | bytes 25165824 | tf_op jit(solution)/shard_map/all_to_all | solution.py:89
  59.4 160.7 %all-to-all-done.1 = f32[32,3,2,128,128]{4,3,2,1,0:T(8,128)} async-done(((f32[32,3,2,128,128]{4,3,2,1,0:T(8,128)}), f32[32,3,2,128,128]{4,3,2,1,0:T(8,128)}, u32[]{:S(2)}, u32[]{:S(2)}) %all-to-all-start.1) | async-done | bytes 12582944 | tf_op jit(solution)/shard_map/all_to_all | solution.py:89
  220.1 202.3 %while.11 = (s32[]{:T(128)}, f32[3,256,256]{2,1,0:T(8,128)S(1)}, f32[12,8,11]{2,1,0:T(8,128)S(1)}, f32[8,2,41]{2,0,1:T(8,128)S(1)}, f32[12,8,2,128,128]{4,3,2,1,0:T(8,128)}, /*index=5*/s32[]{:T(128)}, s32[]{:T(128)}) while((s32[]{:T(128)}, f32[3,256,256]{2,1,0:T(8,128)S(1)}, f32[12,8,11]{2,1,0:T(8,128)S(1)}, ...), condition=%wide.region_10.11_spmd.clone, body=%wide.region_4.10_spmd.clone.sunk | while | flops 4022007040 | bytes 30721944 | solution.py:105
  221.9 1.3 copy_bitcast_fusion.2
  223.2 1.7 fusion.95
  226.2 2.3 fusion.96
  228.6 2.2 fusion.97
  230.8 4.0 fusion.98
  238.8 1.3 copy_bitcast_fusion.2
  240.1 1.7 fusion.95
  243.1 2.3 fusion.96
  245.4 2.2 fusion.97
  247.7 4.0 fusion.98
  255.6 1.3 copy_bitcast_fusion.2
  256.9 1.7 fusion.95
  259.9 2.3 fusion.96
  262.3 2.2 fusion.97
  264.5 4.0 fusion.98
  272.5 1.3 copy_bitcast_fusion.2
  273.8 1.7 fusion.95
  276.8 2.3 fusion.96
  279.1 2.2 fusion.97
  281.4 4.0 fusion.98
  289.4 1.3 copy_bitcast_fusion.2
  290.7 1.7 fusion.95
  293.7 2.3 fusion.96
  296.0 2.2 fusion.97
  298.2 4.0 fusion.98
  306.2 1.3 copy_bitcast_fusion.2
  307.5 1.7 fusion.95
  310.5 2.3 fusion.96
  312.9 2.2 fusion.97
  315.1 4.0 fusion.98
  324.4 1.7 fusion.95
  327.4 2.3 fusion.96
  329.7 2.2 fusion.97
  332.0 4.0 fusion.98
  341.2 1.7 fusion.95
  344.2 2.3 fusion.96
  346.6 2.2 fusion.97
  348.8 4.0 fusion.98
  358.1 1.7 fusion.95
  361.1 2.3 fusion.96
  363.4 2.2 fusion.97
  365.7 4.0 fusion.98
  375.0 1.7 fusion.95
  377.9 2.3 fusion.96
  380.3 2.2 fusion.97
  382.5 4.0 fusion.98
  391.8 1.7 fusion.95
  394.8 2.3 fusion.96
  397.1 2.2 fusion.97
  399.4 4.0 fusion.98
  408.7 1.7 fusion.95
  411.7 2.3 fusion.96
  414.0 2.2 fusion.97
  416.3 4.0 fusion.98
  423.3 40.9 %all-reduce.2.cloned.1.call-done = f32[3,256,256]{2,1,0:T(8,128)} async-done(((f32[3,256,256]{2,1,0:T(8,128)}), f32[3,256,256]{2,1,0:T(8,128)}) %all-reduce.2.cloned.1.call-update) | async-done | bytes 786448 | tf_op jit(solution)/shard_map/psum | solution.py:106
  464.2 2.0 fusion.48
  (268 shorter events, 79.1 us)
Async XLA Ops:
  7.2 4.6 copy-start.6
  7.2 5.6 %copy-start.3 = (f32[32,2,2]{0,2,1:T(2,128)S(1)}, f32[32,2,2]{0,2,1:T(2,128)}, u32[]{:S(2)}) copy-start(f32[32,2,2]{0,2,1:T(2,128)} %param.14) | copy-start | bytes 1540
  7.2 6.5 %copy-start.4 = (f32[32,3]{0,1:T(4,128)S(1)}, f32[32,3]{0,1:T(4,128)}, u32[]{:S(2)}) copy-start(f32[32,3]{0,1:T(4,128)} %param.16) | copy-start | bytes 1156
  8.5 6.1 %copy-start.5 = (s32[32,3]{0,1:T(4,128)S(1)}, s32[32,3]{0,1:T(4,128)}, u32[]{:S(2)}) copy-start(s32[32,3]{0,1:T(4,128)} %param.15) | copy-start | bytes 1156
  10.4 14.5 %copy-start.1 = (f32[32,128,128]{2,1,0:T(8,128)S(1)}, f32[32,128,128]{2,1,0:T(8,128)}, u32[]{:S(2)}) copy-start(f32[32,128,128]{2,1,0:T(8,128)} %param.11) | copy-start | bytes 6291460
  16.5 35.1 %all-to-all-start = ((f32[32,3,11]{2,1,0:T(4,128)}), f32[32,3,11]{2,1,0:T(4,128)S(1)}, u32[]{:S(2)}, u32[]{:S(2)}) async-start(f32[32,3,11]{2,1,0:T(4,128)} %copy.90), calls=%async_computation | async-start | bytes 131072 | tf_op jit(solution)/shard_map/all_to_all | solution.py:90
  51.6 7.7 %copy-start.2 = (f32[8,2,41]{2,1,0:T(2,128)S(1)}, f32[8,2,41]{2,1,0:T(2,128)}, u32[]{:S(2)}) copy-start(f32[8,2,41]{2,1,0:T(2,128)} %param.17) | copy-start | bytes 7876
  51.6 168.5 %all-to-all-start.1 = ((f32[32,3,2,128,128]{4,3,2,1,0:T(8,128)}), f32[32,3,2,128,128]{4,3,2,1,0:T(8,128)}, u32[]{:S(2)}, u32[]{:S(2)}) async-start(f32[32,3,2,128,128]{4,3,2,1,0:T(8,128)} %broadcast_multiply_fusion), calls=%async_computation.1 | async-start | bytes 25165824 | tf_op jit(solution)/shard_map/all_to_all | solution.py:89
  59.3 404.9 %all-reduce.2.cloned.1.call-start = ((), (), s32[]{:S(2)}) async-start(), calls=%async_computation.2 | async-start | bytes 1572864 | tf_op jit(solution)/shard_map/psum | solution.py:106
  422.4 0.9 copy-start
Sparse Core Ops, SparseCore 0:
  423.5 40.6 all-reduce.1
where the time goes:
time: 474 us; the launch traced here: 473 us
  waiting for transfers between devices  202 us (43%)
  matrix products  153 us (32%)
  other arithmetic  47.6 us (10%)
  local copies, waits for them, and re-layouts  38.4 us (8%)
  starting transfers between devices  16.1 us (3%)
  between operations  14.3 us (3%)
    all_to_all x1, waiting for transfers between devices, shards(): lax.all_to_all(sent, 'patch', split_axis=0, concat_axis=0, tiled=True)  161 us
    dot_general x12, matrix products, warp_group(): both = jnp.einsum('gcpj,gqj->gcpq', left, cols_w, precision=HI)  47.7 us
    psum x1, waiting for transfers between devices, shards(): total = lax.psum(partial_value, 'visit')  40.9 us
    dot_general x12, matrix products, convolve(): return jnp.einsum('gbil,gbjl->gij', scaled, col_mats, precision=HI)  27.4 us
    dot_general x12, matrix products, warp_group(): left = jnp.einsum('gpi,gcij->gcpj', rows_w, planes, precision=HI)  26.9 us
    dot_general x12, matrix products, convolve(): partial_rows = jnp.einsum('gbik,gkl->gbil', row_mats, images, precision=HI)  20 us
    squeeze x24, local copies, waits for them, and re-layouts, shards(): partial_value = lax.scan(accumulate, start, (arrived, arrived_meta))[0]  15.7 us
    reduce_sum x12, other arithmetic, warp_group(): cover = jnp.sum(rows_w, 2)[:, :, None] * jnp.sum(cols_w, 2)[:, None, :]  15.5 us
  transfers between devices with their start and end apart: 3, of which 2 were waited for; matrix products, arithmetic and copies ran while one was open for 6% of the time, Pallas kernels for 0%

commit v1 on v0

--- a/solution.py
+++ b/solution.py
@@ -103,7 +103,9 @@
 
     start = jnp.zeros((3, PATCH, PATCH), jnp.float32)
     partial_value = lax.scan(accumulate, start, (arrived, arrived_meta))[0]
-    total = lax.psum(partial_value, "visit")
+    total = partial_value
+    for hop in (1, 2):
+        total = total + lax.ppermute(total, "visit", [(dev, dev ^ hop) for dev in range(4)])
     coadd, coadd_var = finish(total[0], total[1], total[2])
     return (coadd, coadd_var)
 

time: 474 us -> 452 us (0.954)
  waiting for transfers between devices: 202 us -> 187 us
  between operations: 14.3 us -> 0.93 us
  starting transfers between devices: 16.1 us -> 21.7 us
    psum x1 -> x0, waiting for transfers between devices: 40.9 us -> none  [shards(): total = lax.psum(partial_value, 'visit')]
    ppermute x0 -> x2, waiting for transfers between devices: none -> 26.3 us  [shards(): lax.ppermute(total, 'visit', [(dev, dev ^ hop) for dev in range(4)])]
    ppermute x0 -> x2, starting transfers between devices: none -> 5.65 us  [shards(): lax.ppermute(total, 'visit', [(dev, dev ^ hop) for dev in range(4)])]
  transfers between devices with their start and end apart: 3 -> 4, of which waited for: 2 -> 3; matrix products, arithmetic and copies ran while one was open for 6% -> 6% of each run, Pallas kernels for 0% -> 0%
where the time goes in v1:
time: 452 us; the launch traced here: 449 us
  waiting for transfers between devices  187 us (41%)
  matrix products  153 us (34%)
  other arithmetic  46.7 us (10%)
  local copies, waits for them, and re-layouts  37.5 us (8%)
  starting transfers between devices  21.7 us (5%)
    all_to_all x1, waiting for transfers between devices, shards(): lax.all_to_all(sent, 'patch', split_axis=0, concat_axis=0, tiled=True)  161 us
    dot_general x12, matrix products, warp_group(): both = jnp.einsum('gcpj,gqj->gcpq', left, cols_w, precision=HI)  47.7 us
    dot_general x12, matrix products, convolve(): return jnp.einsum('gbil,gbjl->gij', scaled, col_mats, precision=HI)  27.4 us
    dot_general x12, matrix products, warp_group(): left = jnp.einsum('gpi,gcij->gcpj', rows_w, planes, precision=HI)  26.9 us
    ppermute x2, waiting for transfers between devices, shards(): lax.ppermute(total, 'visit', [(dev, dev ^ hop) for dev in range(4)])  26.3 us
    dot_general x12, matrix products, convolve(): partial_rows = jnp.einsum('gbik,gkl->gbil', row_mats, images, precision=HI)  20 us
    squeeze x24, local copies, waits for them, and re-layouts, shards(): partial_value = lax.scan(accumulate, start, (arrived, arrived_meta))[0]  15.7 us
    reduce_sum x12, other arithmetic, warp_group(): cover = jnp.sum(rows_w, 2)[:, :, None] * jnp.sum(cols_w, 2)[:, None, :]  15.5 us
  transfers between devices with their start and end apart: 4, of which 3 were waited for; matrix products, arithmetic and copies ran while one was open for 6% of the time, Pallas kernels for 0%

profile of v1, /device:TPU:0, one launch (start us, length us, event | category | flops | bytes accessed | tf_op | source)
XLA Modules:
  0.0 448.9 jit_solution(15638800382077173973)
XLA Ops:
  2.0 1.9 reduce_sum.75
  10.0 8.4 %all-to-all-start = ((f32[32,3,11]{2,1,0:T(4,128)}), f32[32,3,11]{2,1,0:T(4,128)S(1)}, u32[]{:S(2)}, u32[]{:S(2)}) async-start(f32[32,3,11]{2,1,0:T(4,128)} %copy.90), calls=%async_computation | async-start | bytes 131072 | tf_op jit(solution)/shard_map/all_to_all | solution.py:90
  18.4 3.9 pad_maximum_fusion.1
  22.3 10.9 %gather_fusion.5 = f32[96,2,128,128]{3,2,1,0:T(8,128)} fusion(f32[32,2,128,128]{3,2,0,1:T(8,128)} %pad_maximum_fusion.1, s32[1024]{0:T(1024)S(1)} %get-tuple-element.97), kind=kCustom, calls=%fused_computation.5 | custom fusion | bytes 25166208 | tf_op jit(solution)/shard_map/gather | solution.py:83
  33.3 11.8 %broadcast_multiply_fusion = f32[32,3,2,128,128]{4,3,2,1,0:T(8,128)} fusion(f32[32,3,2,128,128]{4,3,2,1,0:T(8,128)} %bitcast.135, f32[32,3]{1,0:T(8,128)S(1)} %reshape.285), kind=kLoop, calls=%fused_computation.74 | loop fusion | flops 3145728 | bytes 25166208 | tf_op jit(solution)/shard_map/mul | solution.py:83
  45.1 7.6 %all-to-all-start.1 = ((f32[32,3,2,128,128]{4,3,2,1,0:T(8,128)}), f32[32,3,2,128,128]{4,3,2,1,0:T(8,128)}, u32[]{:S(2)}, u32[]{:S(2)}) async-start(f32[32,3,2,128,128]{4,3,2,1,0:T(8,128)} %broadcast_multiply_fusion), calls=%async_computation.1 | async-start | bytes 25165824 | tf_op jit(solution)/shard_map/all_to_all | solution.py:89
  52.8 160.8 %all-to-all-done.1 = f32[32,3,2,128,128]{4,3,2,1,0:T(8,128)} async-done(((f32[32,3,2,128,128]{4,3,2,1,0:T(8,128)}), f32[32,3,2,128,128]{4,3,2,1,0:T(8,128)}, u32[]{:S(2)}, u32[]{:S(2)}) %all-to-all-start.1) | async-done | bytes 12582944 | tf_op jit(solution)/shard_map/all_to_all | solution.py:89
  213.6 202.3 %while.11 = (s32[]{:T(128)}, f32[3,256,256]{2,1,0:T(8,128)S(1)}, f32[12,8,11]{2,1,0:T(8,128)S(1)}, f32[8,2,41]{2,0,1:T(8,128)S(1)}, f32[12,8,2,128,128]{4,3,2,1,0:T(8,128)}, /*index=5*/s32[]{:T(128)}, s32[]{:T(128)}) while((s32[]{:T(128)}, f32[3,256,256]{2,1,0:T(8,128)S(1)}, f32[12,8,11]{2,1,0:T(8,128)S(1)}, ...), condition=%wide.region_10.11_spmd.clone, body=%wide.region_4.10_spmd.clone.sunk | while | flops 4022007040 | bytes 30721944 | solution.py:105
  215.4 1.3 copy_bitcast_fusion.2
  216.7 1.7 fusion.95
  219.7 2.3 fusion.96
  222.0 2.2 fusion.97
  224.3 4.0 fusion.98
  232.2 1.3 copy_bitcast_fusion.2
  233.6 1.7 fusion.95
  236.5 2.3 fusion.96
  238.9 2.2 fusion.97
  241.1 4.0 fusion.98
  249.1 1.3 copy_bitcast_fusion.2
  250.4 1.7 fusion.95
  253.4 2.3 fusion.96
  255.7 2.2 fusion.97
  258.0 4.0 fusion.98
  266.0 1.3 copy_bitcast_fusion.2
  267.3 1.7 fusion.95
  270.3 2.3 fusion.96
  272.6 2.2 fusion.97
  274.8 4.0 fusion.98
  284.1 1.7 fusion.95
  287.1 2.3 fusion.96
  289.5 2.2 fusion.97
  291.7 4.0 fusion.98
  301.0 1.7 fusion.95
  304.0 2.3 fusion.96
  306.3 2.2 fusion.97
  308.6 4.0 fusion.98
  317.8 1.7 fusion.95
  320.8 2.3 fusion.96
  323.2 2.2 fusion.97
  325.4 4.0 fusion.98
  334.7 1.7 fusion.95
  337.7 2.3 fusion.96
  340.0 2.2 fusion.97
  342.3 4.0 fusion.98
  351.6 1.7 fusion.95
  354.6 2.3 fusion.96
  356.9 2.2 fusion.97
  359.1 4.0 fusion.98
  368.4 1.7 fusion.95
  371.4 2.3 fusion.96
  373.8 2.2 fusion.97
  376.0 4.0 fusion.98
  385.3 1.7 fusion.95
  388.3 2.3 fusion.96
  390.6 2.2 fusion.97
  392.9 4.0 fusion.98
  402.1 1.7 fusion.95
  405.1 2.3 fusion.96
  407.5 2.2 fusion.97
  409.7 4.0 fusion.98
  415.9 1.6 collective-permute-start
  417.4 16.3 %collective-permute-done = f32[3,256,256]{2,1,0:T(8,128)S(1)} collective-permute-done((f32[3,256,256]{2,1,0:T(8,128)S(1)}, f32[3,256,256]{2,1,0:T(8,128)S(1)}, u32[]{:S(2)}, u32[]{:S(2)}) %collective-permute-start) | collective-permute-done | bytes 786464 | tf_op jit(solution)/shard_map/ppermute | solution.py:108
  433.9 4.1 collective-permute-start.1
  438.0 10.0 %collective-permute-done.1 = f32[3,256,256]{2,1,0:T(8,128)S(1)} collective-permute-done((f32[3,256,256]{2,1,0:T(8,128)S(1)}, f32[3,256,256]{2,1,0:T(8,128)S(1)}, u32[]{:S(2)}, u32[]{:S(2)}) %collective-permute-start.1) | collective-permute-done | bytes 786464 | tf_op jit(solution)/shard_map/ppermute | solution.py:108
  (269 shorter events, 81.8 us)
Async XLA Ops:
  0.6 4.6 %copy-start.5 = (s32[32,2,2]{0,2,1:T(2,128)S(1)}, s32[32,2,2]{0,2,1:T(2,128)}, u32[]{:S(2)}) copy-start(s32[32,2,2]{0,2,1:T(2,128)} %param.13) | copy-start | bytes 1540
  0.6 5.6 %copy-start.2 = (f32[32,2,2]{0,2,1:T(2,128)S(1)}, f32[32,2,2]{0,2,1:T(2,128)}, u32[]{:S(2)}) copy-start(f32[32,2,2]{0,2,1:T(2,128)} %param.14) | copy-start | bytes 1540
  0.7 6.5 %copy-start.3 = (f32[32,3]{0,1:T(4,128)S(1)}, f32[32,3]{0,1:T(4,128)}, u32[]{:S(2)}) copy-start(f32[32,3]{0,1:T(4,128)} %param.16) | copy-start | bytes 1156
  1.9 6.1 %copy-start.4 = (s32[32,3]{0,1:T(4,128)S(1)}, s32[32,3]{0,1:T(4,128)}, u32[]{:S(2)}) copy-start(s32[32,3]{0,1:T(4,128)} %param.15) | copy-start | bytes 1156
  3.9 14.5 %copy-start = (f32[32,128,128]{2,1,0:T(8,128)S(1)}, f32[32,128,128]{2,1,0:T(8,128)}, u32[]{:S(2)}) copy-start(f32[32,128,128]{2,1,0:T(8,128)} %param.11) | copy-start | bytes 6291460
  10.0 35.1 %all-to-all-start = ((f32[32,3,11]{2,1,0:T(4,128)}), f32[32,3,11]{2,1,0:T(4,128)S(1)}, u32[]{:S(2)}, u32[]{:S(2)}) async-start(f32[32,3,11]{2,1,0:T(4,128)} %copy.90), calls=%async_computation | async-start | bytes 131072 | tf_op jit(solution)/shard_map/all_to_all | solution.py:90
  45.1 7.6 %copy-start.1 = (f32[8,2,41]{2,1,0:T(2,128)S(1)}, f32[8,2,41]{2,1,0:T(2,128)}, u32[]{:S(2)}) copy-start(f32[8,2,41]{2,1,0:T(2,128)} %param.17) | copy-start | bytes 7876
  45.1 168.5 %all-to-all-start.1 = ((f32[32,3,2,128,128]{4,3,2,1,0:T(8,128)}), f32[32,3,2,128,128]{4,3,2,1,0:T(8,128)}, u32[]{:S(2)}, u32[]{:S(2)}) async-start(f32[32,3,2,128,128]{4,3,2,1,0:T(8,128)} %broadcast_multiply_fusion), calls=%async_computation.1 | async-start | bytes 25165824 | tf_op jit(solution)/shard_map/all_to_all | solution.py:89
  415.9 17.9 %collective-permute-start = (f32[3,256,256]{2,1,0:T(8,128)S(1)}, f32[3,256,256]{2,1,0:T(8,128)S(1)}, u32[]{:S(2)}, u32[]{:S(2)}) collective-permute-start(f32[3,256,256]{2,1,0:T(8,128)S(1)} %get-tuple-element.29), channel_id=1, source_target_pairs={{0,32},{32,0},{64,96},{96,64},{1,33},{33,1},{65,97},{97,65},{2,34}... | collective-permute-start | bytes 2359304 | tf_op jit(solution)/shard_map/ppermute | solution.py:108
  433.9 14.1 %collective-permute-start.1 = (f32[3,256,256]{2,1,0:T(8,128)S(1)}, f32[3,256,256]{2,1,0:T(8,128)S(1)}, u32[]{:S(2)}, u32[]{:S(2)}) collective-permute-start(f32[3,256,256]{2,1,0:T(8,128)S(1)} %add.63), channel_id=1, source_target_pairs={{0,64},{32,96},{64,0},{96,32},{1,65},{33,97},{65,1},{97,33},{2,66}... | collective-permute-start | bytes 2359304 | tf_op jit(solution)/shard_map/ppermute | solution.py:108
